TPU v7x, 256 devices: a whole 4x4x8 slice. The times are simulated.
256 devices in a mesh: req: 32 (over z, x), mlp: 8 (over y, core).
Axes of the slice: x: 4, y: 4, z: 8, core: 2. Of those that a mesh axis runs over, the one named last changes fastest.
Arguments:
- tokens: bfloat16 [8192, 2048], P('req', 'mlp'), may hold values from -12 to 12
- segment_ids: int32 [8192], P('req'), may hold values from 0 to 16, never falling along the last dimension, each value on 1 to 4096 neighbouring positions
- page_source: int32 [512], P('req'), may hold values from 0 to 511, each once
- query_weight: bfloat16 [2048, 2048], P(None, 'mlp')
- key_weight: bfloat16 [2048, 2048], P(None, 'mlp')
- value_weight: bfloat16 [2048, 2048], P(None, 'mlp'), may hold values from -0.125 to 0.125
- out_weight: bfloat16 [2048, 2048], P('mlp')
- query_gain: float32 [2048], P('mlp'), may hold values from 0.5 to 9
- key_gain: float32 [2048], P('mlp'), may hold values from 0.5 to 9
- attention_gain: float32 [2048], P('mlp'), may hold values from 0.25 to 1.75
- gate_weight: bfloat16 [2048, 8192], P('req', 'mlp'), may hold values from -0.125 to 0.125
- up_weight: bfloat16 [2048, 8192], P('req', 'mlp'), may hold values from -0.125 to 0.125
- down_weight: bfloat16 [2048, 8192], P('req', 'mlp')
- feedforward_gain: float32 [2048], P('mlp'), may hold values from 0.25 to 1.75
Outputs:
- layer_out: bfloat16 [8192, 2048], P('req', 'mlp')
- page_cache: bfloat16 [512, 2, 16, 2048], P('req', None, None, 'mlp')
Inputs may be any that keep to these rules, and one draw needn't show every extreme that they name: `segment_ids`: segment ids never fall along the stream; each prompt has 1 to 4096 tokens and one has exactly 4096. `page_source`: each stream page appears once.
All inputs are finite; a program needn't handle non-finite values.
Results may differ from a plain program's by a relative error of at most 0.019.
The roundings to bfloat16 on the way count: a program that leaves them out, or rounds other values in their place, can miss the bound.
Values may be sent and summed in bfloat16 or wider, within the bound.
No kernel may reach another device: no remote copies, remote signals or barrier semaphores. Data moves between devices by JAX's collectives and lax.ppermute only.
A program may use at most 128 MiB of HBM per device.

v0:
```python
import jax
import jax.numpy as jnp
from jax import lax
from jax.sharding import PartitionSpec as P

HD = 128
PAGE = 16
rope_base = 500000.0
norm_eps = 1e-06


def rope_tables(positions, head_dim):
    half_dim = head_dim // 2
    inv_freq = rope_base ** (-(jnp.arange(half_dim, dtype=jnp.float32) * 2.0) / head_dim)
    angles = positions.astype(jnp.float32)[:, None] * inv_freq[None, :]
    return (jnp.cos(angles), jnp.sin(angles))


def rotate(values, cosine_table, sine_table, head_dim):
    tok_rows = values.shape[0]
    head_count = values.shape[1] // head_dim
    shaped = values.reshape(tok_rows, head_count, head_dim)
    half_dim = head_dim // 2
    first_half = shaped[..., :half_dim]
    second = shaped[..., half_dim:]
    cos_b = cosine_table[:, None, :]
    sin_b = sine_table[:, None, :]
    turned = jnp.concatenate(
        [first_half * cos_b - second * sin_b, second * cos_b + first_half * sin_b], axis=-1
    )
    return turned.reshape(tok_rows, head_count * head_dim)


def post_norm(branch_term, gain_vec, model_width):
    own_part = lax.psum_scatter(
        branch_term.astype(jnp.bfloat16), "mlp", scatter_dimension=1, tiled=True
    ).astype(jnp.float32)
    mean_square = lax.psum(jnp.sum(own_part * own_part, axis=1), "mlp") / model_width
    return own_part * lax.rsqrt(mean_square + norm_eps)[:, None] * gain_vec[None, :]


def per_device(
    tokens,
    segment_ids,
    page_source,
    query_weight,
    key_weight,
    value_weight,
    out_weight,
    query_gain,
    key_gain,
    attention_gain,
    gate_weight,
    up_weight,
    down_weight,
    feedforward_gain,
):
    tok_rows = tokens.shape[0]
    local_width = tokens.shape[1]
    model_width = query_weight.shape[0]
    head_dim = HD
    head_count = local_width // head_dim
    full_rows = lax.all_gather(tokens, "mlp", axis=1, tiled=True)
    query_proj = jnp.dot(full_rows, query_weight, preferred_element_type=jnp.float32)
    key_proj = jnp.dot(full_rows, key_weight, preferred_element_type=jnp.float32)
    value_proj = jnp.dot(full_rows, value_weight, preferred_element_type=jnp.float32)
    query_total, key_total = lax.psum(
        (jnp.sum(query_proj * query_proj, axis=1), jnp.sum(key_proj * key_proj, axis=1)), "mlp"
    )
    query_n = (
        query_proj * lax.rsqrt(query_total / model_width + norm_eps)[:, None] * query_gain[None, :]
    )
    key_n = key_proj * lax.rsqrt(key_total / model_width + norm_eps)[:, None] * key_gain[None, :]
    seg_total = lax.axis_size("req") // 2 + 1
    seg_range = jnp.arange(seg_total, dtype=jnp.int32)
    matches = segment_ids[:, None] == seg_range[None, :]
    counts = jnp.sum(matches.astype(jnp.int32), axis=0)
    totals = lax.psum(counts, "req")
    seg_starts = jnp.cumsum(totals) - totals
    row_base = lax.axis_index("req") * tok_rows
    global_index = row_base + jnp.arange(tok_rows, dtype=jnp.int32)
    own_start = jnp.sum(jnp.where(matches, seg_starts[None, :], 0), axis=1)
    positions = global_index - own_start
    cosine_table, sine_table = rope_tables(positions, head_dim)
    query_r = rotate(query_n, cosine_table, sine_table, head_dim).astype(jnp.bfloat16)
    key_r = rotate(key_n, cosine_table, sine_table, head_dim).astype(jnp.bfloat16)
    value_b = value_proj.astype(jnp.bfloat16)
    query_heads = query_r.reshape(tok_rows, head_count, head_dim)
    score_scale = head_dim ** (-0.5)
    pages_here = page_source.shape[0]
    page_offsets = jnp.arange(PAGE, dtype=jnp.int32)
    attn_init = (
        jnp.full((head_count, tok_rows), -1e30, jnp.float32),
        jnp.zeros((head_count, tok_rows), jnp.float32),
        jnp.zeros((tok_rows, head_count, head_dim), jnp.float32),
    )
    cache_init = jnp.zeros((pages_here, 2, PAGE, local_width), jnp.bfloat16)
    fold_state = attn_init + (cache_init,)
    fetched = (
        lax.all_gather(key_r, "req", axis=0, tiled=True),
        lax.all_gather(value_b, "req", axis=0, tiled=True),
        lax.all_gather(segment_ids, "req", axis=0, tiled=True),
    )
    key_part, value_part, seg_part = fetched
    row_count = key_part.shape[0]
    block_rows = 512

    def one_block(block_index, state):
        run_max, run_sum, run_out = state
        offset = block_index * block_rows
        key_block = lax.dynamic_slice_in_dim(key_part, offset, block_rows, 0).reshape(
            block_rows, head_count, head_dim
        )
        value_block = lax.dynamic_slice_in_dim(value_part, offset, block_rows, 0).reshape(
            block_rows, head_count, head_dim
        )
        seg_block = lax.dynamic_slice_in_dim(seg_part, offset, block_rows, 0)
        key_index = offset + jnp.arange(block_rows, dtype=jnp.int32)
        visible = (
            (segment_ids[:, None] == seg_block[None, :])
            & (global_index[:, None] >= key_index[None, :])
            & (key_index[None, :] >= 0)
        )
        scores = (
            jnp.einsum("thd,rhd->htr", query_heads, key_block, preferred_element_type=jnp.float32)
            * score_scale
        )
        masked = jnp.where(visible[None], scores, -1e30)
        new_max = jnp.maximum(run_max, jnp.max(masked, axis=2))
        weights = jnp.where(visible[None], jnp.exp(scores - new_max[:, :, None]), 0.0)
        factor = jnp.exp(run_max - new_max)
        run_sum = run_sum * factor + jnp.sum(weights, axis=2)
        update = jnp.einsum(
            "htr,rhd->thd",
            weights.astype(jnp.bfloat16),
            value_block,
            preferred_element_type=jnp.float32,
        )
        run_out = run_out * factor.T[:, :, None] + update
        return (new_max, run_sum, run_out)

    attn_state = lax.fori_loop(0, row_count // block_rows, one_block, fold_state[:3])
    place_key_part = fetched[0]
    row_count = place_key_part.shape[0]
    page_rows = page_source[:, None] * PAGE + page_offsets[None, :]
    in_piece = (page_rows >= 0) & (page_rows < row_count)
    clipped = jnp.clip(page_rows, 0, row_count - 1)
    stacked = jnp.stack([place_key_part[clipped], fetched[1][clipped]], axis=1)
    page_cache = jnp.where(in_piece[:, None, :, None], stacked, fold_state[3])
    run_max, run_sum, run_out, page_cache = (
        attn_state[0],
        attn_state[1],
        attn_state[2],
        page_cache,
    )
    attended = (run_out / run_sum.T[:, :, None]).reshape(tok_rows, local_width).astype(jnp.bfloat16)
    projected = jnp.dot(attended, out_weight, preferred_element_type=jnp.float32)
    residual = (
        tokens.astype(jnp.float32) + post_norm(projected, attention_gain, model_width)
    ).astype(jnp.bfloat16)
    normed = lax.all_gather(residual, "mlp", axis=1, tiled=True)
    contract = (((1,), (1,)), ((), ()))
    fetched = (
        lax.all_gather(gate_weight, "req", axis=0, tiled=True),
        lax.all_gather(up_weight, "req", axis=0, tiled=True),
    )
    gate_act = jnp.dot(normed, fetched[0], preferred_element_type=jnp.float32)
    up_act = jnp.dot(normed, fetched[1], preferred_element_type=jnp.float32)
    hidden = (jax.nn.silu(gate_act) * up_act).astype(jnp.bfloat16)
    down_act = lax.dot_general(
        hidden,
        lax.all_gather(down_weight, "req", axis=0, tiled=True),
        contract,
        preferred_element_type=jnp.float32,
    )
    layer_out = (
        residual.astype(jnp.float32) + post_norm(down_act, feedforward_gain, model_width)
    ).astype(jnp.bfloat16)
    return (layer_out, page_cache)


def solution(mesh):
    in_specs = (
        P("req", "mlp"),
        P("req"),
        P("req"),
        P(None, "mlp"),
        P(None, "mlp"),
        P(None, "mlp"),
        P("mlp", None),
        P("mlp"),
        P("mlp"),
        P("mlp"),
        P("req", "mlp"),
        P("req", "mlp"),
        P("req", "mlp"),
        P("mlp"),
    )
    out_specs = (P("req", "mlp"), P("req", None, None, "mlp"))
    return jax.shard_map(
        per_device, mesh=mesh, in_specs=in_specs, out_specs=out_specs, check_vma=False
    )
```

profile of v0, /device:TPU:1, one launch (start us, length us, event | category | flops | bytes accessed | tf_op | source)
XLA Modules:
  0.0 636.5 jit_solution(3490800853905953545)
XLA Ops:
  7.2 0.7 all-gather.9.cloned.1.call-update
  8.0 0.8 convert_reduce_fusion
  8.8 19.8 %psum.36 = s32[17]{0:T(128)S(1)} all-reduce(s32[17]{0:T(128)S(1)} %convert_reduce_fusion), channel_id=1, replica_groups=mesh['req'=32,'mlp'=8] {'req'}, use_global_device_ids=true, to_apply=%region_3.0 | all-reduce | flops 17 | bytes 136 | tf_op jit(solution)/shard_map/psum | solution.py:78
  28.9 0.8 select_reduce_fusion.1
  29.7 1.2 multiply_cosine_fusion
  30.9 9.1 %all-gather.9.cloned.1.call-done = bf16[256,2048]{1,0:T(8,128)(2,1)} async-done(((bf16[256,256]{1,0:T(8,128)(2,1)}), bf16[256,2048]{1,0:T(8,128)(2,1)}) %all-gather.9.cloned.1.call-update) | async-done | bytes 1048592 | tf_op jit(solution)/shard_map/all_gather | solution.py:63
  40.0 2.1 multiply_reduce_fusion.1
  42.0 2.2 multiply_reduce_fusion
  44.2 12.1 %all-reduce = (f32[256]{0:T(256)S(1)}, f32[256]{0:T(256)S(1)}) all-reduce(f32[256]{0:T(256)S(1)} %get-tuple-element.290, f32[256]{0:T(256)S(1)} %get-tuple-element.292), channel_id=1, replica_groups=mesh['req'=32,'mlp'=8] {'mlp'}, use_global_device_ids=true, to_apply=%region_1.0 | all-reduce | flops 512 | bytes 4096 | tf_op jit(solution)/shard_map/psum | solution.py:67
  57.1 1.1 subtract_convert_fusion
  58.2 0.8 copy_bitcast_fusion
  59.0 2.3 convolution_convert_fusion.2
  61.4 35.7 %all-gather = s32[32,1,256]{2,1,0:T(1,128)S(1)} all-gather(s32[1,1,256]{2,1,0:T(1,128)S(1)} %bitcast.69), channel_id=1, replica_groups=mesh['req'=32,'mlp'=8] {'req'}, dimensions={0}, use_global_device_ids=true | all-gather | bytes 33792 | tf_op jit(solution)/shard_map/all_gather | solution.py:102
  97.3 40.7 %all-gather.11.cloned.1.call-done = bf16[8192,256]{1,0:T(8,128)(2,1)} async-done(((bf16[256,256]{1,0:T(8,128)(2,1)}), bf16[8192,256]{1,0:T(8,128)(2,1)}) %all-gather.11.cloned.1.call-update) | async-done | bytes 4194320 | tf_op jit(solution)/shard_map/all_gather | solution.py:100
  138.0 81.7 %all-gather.13.cloned.1.call-done = bf16[8192,256]{1,0:T(8,128)(2,1)} async-done(((bf16[256,256]{1,0:T(8,128)(2,1)}), bf16[8192,256]{1,0:T(8,128)(2,1)}) %all-gather.13.cloned.1.call-update) | async-done | bytes 4194320 | tf_op jit(solution)/shard_map/all_gather | solution.py:101
  219.7 44.8 %while.18 = (s32[]{:T(128)}, f32[2,256]{1,0:T(2,128)S(1)}, f32[2,256]{1,0:T(2,128)S(1)}, f32[256,2,128]{0,2,1:T(8,128)S(1)}, s32[256]{0:T(256)S(1)}, /*index=5*/...) while((s32[]{:T(128)}, f32[2,256]{1,0:T(2,128)S(1)}, ...), condition=%wide.region_11.12_spmd.clone, body=%wide.region_8.11_spmd.clone.sunk | while | flops 137302784 | bytes 6994131 | solution.py:142
  220.1 1.1 constant_dynamic-slice_fusion.3
  222.9 1.1 constant_dynamic-slice_fusion.3
  224.7 0.4 fusion.63
  225.7 1.1 constant_dynamic-slice_fusion.3
  228.5 1.1 constant_dynamic-slice_fusion.3
  230.3 0.4 fusion.63
  231.3 1.1 constant_dynamic-slice_fusion.3
  234.1 1.1 constant_dynamic-slice_fusion.3
  235.9 0.4 fusion.63
  236.9 1.1 constant_dynamic-slice_fusion.3
  238.7 0.4 fusion.63
  239.7 1.1 constant_dynamic-slice_fusion.3
  241.5 0.4 fusion.63
  242.5 1.1 constant_dynamic-slice_fusion.3
  244.3 0.4 fusion.63
  245.3 1.1 constant_dynamic-slice_fusion.3
  247.1 0.4 fusion.63
  248.1 1.1 constant_dynamic-slice_fusion.3
  249.9 0.4 fusion.63
  250.9 1.1 constant_dynamic-slice_fusion.3
  252.7 0.4 fusion.63
  253.7 1.1 constant_dynamic-slice_fusion.3
  256.5 1.1 constant_dynamic-slice_fusion.3
  258.3 0.4 fusion.63
  259.4 1.1 constant_dynamic-slice_fusion.3
  262.2 1.1 constant_dynamic-slice_fusion.3
  263.9 0.4 fusion.63
  264.6 1.5 convolution_convert_fusion.1
  266.2 0.5 all-gather.17.cloned.1.call-update
  266.8 32.4 %reduce-scatter.3.cloned.1.call-done = bf16[256,256]{1,0:T(8,128)(2,1)} async-done(((bf16[256,2048]{1,0:T(8,128)(2,1)}), bf16[256,256]{1,0:T(8,128)(2,1)}) %reduce-scatter.3.cloned.1.call-update) | async-done | bytes 131088 | tf_op jit(solution)/shard_map/reduce_scatter | solution.py:35
  299.2 1.0 fusion.16
  300.2 14.8 %psum.38 = f32[256]{0:T(256)S(1)} all-reduce(f32[256]{0:T(256)S(1)} %fusion.16), channel_id=1, replica_groups=mesh['req'=32,'mlp'=8] {'mlp'}, use_global_device_ids=true, to_apply=%region_14.15 | all-reduce | flops 256 | bytes 2048 | tf_op jit(solution)/shard_map/psum | solution.py:38
  315.0 1.7 fusion.19
  316.7 0.7 all-gather.19.cloned.1.call-update
  317.5 0.7 all-gather.21.cloned.1.call-update
  318.2 62.7 %all-gather.17.cloned.1.call-done = bf16[2048,1024]{1,0:T(8,128)(2,1)} async-done(((bf16[64,1024]{1,0:T(8,128)(2,1)}), bf16[2048,1024]{1,0:T(8,128)(2,1)}) %all-gather.17.cloned.1.call-update) | async-done | bytes 4194320 | tf_op jit(solution)/shard_map/all_gather | solution.py:164
  380.9 28.9 %all-gather.15.cloned.1.call-done = bf16[256,2048]{1,0:T(8,128)(2,1)} async-done(((bf16[256,256]{1,0:T(8,128)(2,1)}), bf16[256,2048]{1,0:T(8,128)(2,1)}) %all-gather.15.cloned.1.call-update) | async-done | bytes 1048592 | tf_op jit(solution)/shard_map/all_gather | solution.py:161
  409.8 3.8 fusion.31
  413.6 77.5 %all-gather.19.cloned.1.call-done = bf16[2048,1024]{1,0:T(8,128)(2,1)} async-done(((bf16[64,1024]{1,0:T(8,128)(2,1)}), bf16[2048,1024]{1,0:T(8,128)(2,1)}) %all-gather.19.cloned.1.call-update) | async-done | bytes 4194320 | tf_op jit(solution)/shard_map/all_gather | solution.py:165
  491.1 81.2 %all-gather.21.cloned.1.call-done = bf16[2048,1024]{1,0:T(8,128)(2,1)} async-done(((bf16[64,1024]{1,0:T(8,128)(2,1)}), bf16[2048,1024]{1,0:T(8,128)(2,1)}) %all-gather.21.cloned.1.call-update) | async-done | bytes 4194320 | tf_op jit(solution)/shard_map/all_gather | solution.py:172
  572.3 7.1 %convolution_convert_fusion = bf16[256,2048]{1,0:T(8,128)(2,1)} fusion(bf16[2048,1024]{1,0:T(8,128)(2,1)} %all-gather.21.cloned.1.call-done, bf16[256,2048]{1,0:T(8,128)(2,1)S(1)} %copy-done.9, bf16[2048,1024]{1,0:T(8,128)(2,1)} %all-gather.19.cloned.1.call-done, f32[256,1024]{1,0:T(8,128)S(1)} %fusion.31), kind=kOutput, calls=%fused_computation.28 | convolution fusion | flops 2149580800 | bytes 11534336 | tf_op jit(solution)/shard_map/dot_general | solution.py:170
  579.7 3.7 gather_fusion
  583.4 3.7 gather_fusion.1
  587.1 0.8 maximum_select_fusion
  587.9 24.6 %reduce-scatter.5.cloned.1.call-done = bf16[256,256]{1,0:T(8,128)(2,1)} async-done(((bf16[256,2048]{1,0:T(8,128)(2,1)}), bf16[256,256]{1,0:T(8,128)(2,1)}) %reduce-scatter.5.cloned.1.call-update) | async-done | bytes 131088 | tf_op jit(solution)/shard_map/reduce_scatter | solution.py:35
  612.5 1.0 fusion.20
  613.5 14.7 %psum.39 = f32[256]{0:T(256)S(1)} all-reduce(f32[256]{0:T(256)S(1)} %fusion.20), channel_id=1, replica_groups=mesh['req'=32,'mlp'=8] {'mlp'}, use_global_device_ids=true, to_apply=%region_17.18 | all-reduce | flops 256 | bytes 2048 | tf_op jit(solution)/shard_map/psum | solution.py:38
  628.2 1.7 fusion.23
  (260 shorter events, 24.1 us)
Async XLA Ops:
  7.2 257.4 %copy-start = (bf16[256,2048]{1,0:T(8,128)(2,1)S(1)}, bf16[256,2048]{1,0:T(8,128)(2,1)}, u32[]{:S(2)}) copy-start(bf16[256,2048]{1,0:T(8,128)(2,1)} %param.22) | copy-start | bytes 3145732
  7.2 49.1 %copy-start.5 = (f32[256]{0:T(256)S(1)}, f32[256]{0:T(256)}, u32[]{:S(2)}) copy-start(f32[256]{0:T(256)} %param.24) | copy-start | bytes 3076
  7.2 49.5 %copy-start.6 = (f32[256]{0:T(256)S(1)}, f32[256]{0:T(256)}, u32[]{:S(2)}) copy-start(f32[256]{0:T(256)} %param.23) | copy-start | bytes 3076
  7.2 32.8 %all-gather.9.cloned.1.call-start = ((), (), s32[]{:S(2)}) async-start(), calls=%async_computation.2 | async-start | bytes 1179648 | tf_op jit(solution)/shard_map/all_gather | solution.py:63
  7.9 130.0 %all-gather.11.cloned.1.call-start = ((), (), s32[]{:S(2)}) async-start(), calls=%async_computation.3 | async-start | bytes 4325376 | tf_op jit(solution)/shard_map/all_gather | solution.py:100
  42.0 17.0 %copy-start.1 = (bf16[256,2048]{1,0:T(8,128)(2,1)S(1)}, bf16[256,2048]{1,0:T(8,128)(2,1)}, u32[]{:S(2)}) copy-start(bf16[256,2048]{1,0:T(8,128)(2,1)} %all-gather.9.cloned.1.call-done) | copy-start | bytes 3145732
  56.3 5.1 copy-start.4
  58.9 160.8 %all-gather.13.cloned.1.call-start = ((), (), s32[]{:S(2)}) async-start(), calls=%async_computation.4 | async-start | bytes 4325376 | tf_op jit(solution)/shard_map/all_gather | solution.py:101
  61.3 237.8 %reduce-scatter.3.cloned.1.call-start = ((), (), s32[]{:S(2)}) async-start(), calls=%async_computation.5 | async-start | bytes 1179648 | tf_op jit(solution)/shard_map/reduce_scatter | solution.py:35
  219.7 95.2 %copy-start.3 = (bf16[256,256]{1,0:T(8,128)(2,1)S(1)}, bf16[256,256]{1,0:T(8,128)(2,1)}, u32[]{:S(2)}) copy-start(bf16[256,256]{1,0:T(8,128)(2,1)} %param.16) | copy-start | bytes 393220
  219.7 95.2 %copy-start.7 = (f32[256]{0:T(256)S(1)}, f32[256]{0:T(256)}, u32[]{:S(2)}) copy-start(f32[256]{0:T(256)} %param.25) | copy-start | bytes 3076
  266.1 114.8 %all-gather.17.cloned.1.call-start = ((), (), s32[]{:S(2)}) async-start(), calls=%async_computation.7 | async-start | bytes 4325376 | tf_op jit(solution)/shard_map/all_gather | solution.py:164
  266.7 143.0 %all-gather.15.cloned.1.call-start = ((), (), s32[]{:S(2)}) async-start(), calls=%async_computation.6 | async-start | bytes 1179648 | tf_op jit(solution)/shard_map/all_gather | solution.py:161
  316.7 174.5 %all-gather.19.cloned.1.call-start = ((), (), s32[]{:S(2)}) async-start(), calls=%async_computation.8 | async-start | bytes 4325376 | tf_op jit(solution)/shard_map/all_gather | solution.py:165
  317.4 254.9 %all-gather.21.cloned.1.call-start = ((), (), s32[]{:S(2)}) async-start(), calls=%async_computation.9 | async-start | bytes 4325376 | tf_op jit(solution)/shard_map/all_gather | solution.py:172
  318.2 294.3 %reduce-scatter.5.cloned.1.call-start = ((), (), s32[]{:S(2)}) async-start(), calls=%async_computation.10 | async-start | bytes 1179648 | tf_op jit(solution)/shard_map/reduce_scatter | solution.py:35
  409.8 162.5 %copy-start.9 = (bf16[256,2048]{1,0:T(8,128)(2,1)S(1)}, bf16[256,2048]{1,0:T(8,128)(2,1)}, u32[]{:S(2)}) copy-start(bf16[256,2048]{1,0:T(8,128)(2,1)} %all-gather.15.cloned.1.call-done) | copy-start | bytes 3145732
  413.6 165.8 %copy-start.10 = (s32[16]{0:T(128)S(1)}, s32[16]{0:T(128)}, u32[]{:S(2)}) copy-start(s32[16]{0:T(128)} %param.18) | copy-start | bytes 196
  413.6 214.6 %copy-start.8 = (f32[256]{0:T(256)S(1)}, f32[256]{0:T(256)}, u32[]{:S(2)}) copy-start(f32[256]{0:T(256)} %param.29) | copy-start | bytes 3076
  579.4 48.8 %copy-start.2 = (bf16[256,256]{1,0:T(8,128)(2,1)S(1)}, bf16[256,256]{1,0:T(8,128)(2,1)}, u32[]{:S(2)}) copy-start(bf16[256,256]{1,0:T(8,128)(2,1)} %fusion.19) | copy-start | bytes 393220
Sparse Core Ops, SparseCore 0:
  9.8 30.0 all-gather.8
  59.1 78.8 all-gather.10
  141.1 78.5 all-gather.12
  266.3 32.8 reduce-scatter.2
  301.6 79.2 all-gather.16
  383.2 26.5 all-gather.14
  412.3 78.7 all-gather.18
  493.7 78.5 all-gather.20
  579.5 32.8 reduce-scatter.4
where the time goes:
time: 637 us; the launch traced here: 636 us
  waiting for transfers between devices  441 us (69%)
  blocking collectives  97.1 us (15%)
  local copies, waits for them, and re-layouts  31.1 us (5%)
  matrix products  31 us (5%)
  other arithmetic  20.1 us (3%)
  between operations  14.1 us (2%)
    all_gather x1, waiting for transfers between devices, per_device(): lax.all_gather(value_b, 'req', axis=0, tiled=True)  81.7 us
    all_gather x1, waiting for transfers between devices, per_device(): lax.all_gather(down_weight, 'req', axis=0, tiled=True)  81.2 us
    all_gather x1, waiting for transfers between devices, per_device(): lax.all_gather(up_weight, 'req', axis=0, tiled=True)  77.5 us
    all_gather x1, waiting for transfers between devices, per_device(): lax.all_gather(gate_weight, 'req', axis=0, tiled=True)  62.7 us
    reduce_scatter x2, waiting for transfers between devices, post_norm(): lax.psum_scatter(branch_term.astype(jnp.bfloat16), 'mlp', scatter_dimensi...  57 us
    all_gather x1, waiting for transfers between devices, per_device(): lax.all_gather(key_r, 'req', axis=0, tiled=True)  40.7 us
    all_gather x1, blocking collectives, per_device(): lax.all_gather(segment_ids, 'req', axis=0, tiled=True)  35.7 us
    psum x2, blocking collectives, post_norm(): lax.psum(jnp.sum(own_part * own_part, axis=1), 'mlp') / model_width  29.5 us
  transfers between devices with their start and end apart: 9, of which 9 were waited for; matrix products, arithmetic and copies ran while one was open for 3% of the time, Pallas kernels for 0%

commit v1 on v0

--- a/solution.py
+++ b/solution.py
@@ -158,7 +158,32 @@
     residual = (
         tokens.astype(jnp.float32) + post_norm(projected, attention_gain, model_width)
     ).astype(jnp.bfloat16)
-    normed = lax.all_gather(residual, "mlp", axis=1, tiled=True)
+
+    def reach_panels_here(packet, mesh_name):
+        prior, plain, mixed_arr = (
+            lax.psum(1, mesh_name),
+            lax.axis_index(mesh_name),
+            packet.shape[1],
+        )
+        crops = [(m, (m + 1) % prior) for m in range(prior)]
+        buffers = [(m, (m - 1) % prior) for m in range(prior)]
+        before = jnp.zeros((*packet.shape[:1], prior * mixed_arr, *packet.shape[2:]), packet.dtype)
+        all_values = h_now = packet
+        upper = prior // 2
+        before = lax.dynamic_update_slice_in_dim(before, packet, plain * mixed_arr, axis=1)
+        for p in range(1, upper + 1):
+            all_values = lax.ppermute(all_values, mesh_name, crops)
+            before = lax.dynamic_update_slice_in_dim(
+                before, all_values, (plain - p) % prior * mixed_arr, axis=1
+            )
+            if p < prior - upper:
+                h_now = lax.ppermute(h_now, mesh_name, buffers)
+                before = lax.dynamic_update_slice_in_dim(
+                    before, h_now, (plain + p) % prior * mixed_arr, axis=1
+                )
+        return before
+
+    normed = reach_panels_here(residual, "mlp")
     contract = (((1,), (1,)), ((), ()))
     fetched = (
         lax.all_gather(gate_weight, "req", axis=0, tiled=True),

time: 637 us -> 608 us (0.954)
  waiting for transfers between devices: 441 us -> 403 us
  starting transfers between devices: 0.36 us -> 10.2 us
    all_gather x1 -> x0, waiting for transfers between devices: 28.9 us -> none  [per_device(): normed = lax.all_gather(residual, 'mlp', axis=1, tiled=True)]
    all_gather x1, waiting for transfers between devices: 62.7 us -> 45.7 us  [per_device(): lax.all_gather(gate_weight, 'req', axis=0, tiled=True)]
    ppermute x0 -> x7, starting transfers between devices: none -> 9.86 us  [the longest x3 6.69 us: reach_panels_here(): h_now = lax.ppermute(h_now, mesh_name, buffers)]
    ppermute x0 -> x7, waiting for transfers between devices: none -> 9.05 us  [the longest x4 7.57 us: reach_panels_here(): all_values = lax.ppermute(all_values, mesh_name, crops)]
  transfers between devices with their start and end apart: 9 -> 15, of which waited for: 9 -> 15; matrix products, arithmetic and copies ran while one was open for 3% -> 3% of each run, Pallas kernels for 0% -> 0%
where the time goes in v1:
time: 608 us; the launch traced here: 607 us
  waiting for transfers between devices  403 us (66%)
  blocking collectives  97.3 us (16%)
  local copies, waits for them, and re-layouts  31.3 us (5%)
  matrix products  30.4 us (5%)
  other arithmetic  19.4 us (3%)
  between operations  14.5 us (2%)
  starting transfers between devices  10.2 us (2%)
    all_gather x1, waiting for transfers between devices, per_device(): lax.all_gather(value_b, 'req', axis=0, tiled=True)  81.7 us
    all_gather x1, waiting for transfers between devices, per_device(): lax.all_gather(down_weight, 'req', axis=0, tiled=True)  81.2 us
    all_gather x1, waiting for transfers between devices, per_device(): lax.all_gather(up_weight, 'req', axis=0, tiled=True)  77.5 us
    reduce_scatter x2, waiting for transfers between devices, post_norm(): lax.psum_scatter(branch_term.astype(jnp.bfloat16), 'mlp', scatter_dimensi...  55.5 us
    all_gather x1, waiting for transfers between devices, per_device(): lax.all_gather(gate_weight, 'req', axis=0, tiled=True)  45.7 us
    all_gather x1, waiting for transfers between devices, per_device(): lax.all_gather(key_r, 'req', axis=0, tiled=True)  40.7 us
    all_gather x1, blocking collectives, per_device(): lax.all_gather(segment_ids, 'req', axis=0, tiled=True)  35.7 us
    psum x2, blocking collectives, post_norm(): lax.psum(jnp.sum(own_part * own_part, axis=1), 'mlp') / model_width  29.7 us
  transfers between devices with their start and end apart: 15, of which 15 were waited for; matrix products, arithmetic and copies ran while one was open for 3% of the time, Pallas kernels for 0%

profile of v1, /device:TPU:1, one launch (start us, length us, event | category | flops | bytes accessed | tf_op | source)
XLA Modules:
  0.0 607.4 jit_solution(18120549850336110858)
XLA Ops:
  7.2 0.7 all-gather.8.cloned.1.call-update
  8.0 0.8 convert_reduce_fusion
  8.8 19.8 %psum.36 = s32[17]{0:T(128)S(1)} all-reduce(s32[17]{0:T(128)S(1)} %convert_reduce_fusion), channel_id=1, replica_groups=mesh['req'=32,'mlp'=8] {'req'}, use_global_device_ids=true, to_apply=%region_3.0 | all-reduce | flops 17 | bytes 136 | tf_op jit(solution)/shard_map/psum | solution.py:78
  28.9 0.8 select_reduce_fusion.1
  29.7 1.2 multiply_cosine_fusion
  30.9 9.1 %all-gather.8.cloned.1.call-done = bf16[256,2048]{1,0:T(8,128)(2,1)} async-done(((bf16[256,256]{1,0:T(8,128)(2,1)}), bf16[256,2048]{1,0:T(8,128)(2,1)}) %all-gather.8.cloned.1.call-update) | async-done | bytes 1048592 | tf_op jit(solution)/shard_map/all_gather | solution.py:63
  40.0 2.1 multiply_reduce_fusion.1
  42.0 2.2 multiply_reduce_fusion
  44.2 12.1 %all-reduce = (f32[256]{0:T(256)S(1)}, f32[256]{0:T(256)S(1)}) all-reduce(f32[256]{0:T(256)S(1)} %get-tuple-element.292, f32[256]{0:T(256)S(1)} %get-tuple-element.294), channel_id=1, replica_groups=mesh['req'=32,'mlp'=8] {'mlp'}, use_global_device_ids=true, to_apply=%region_1.0 | all-reduce | flops 512 | bytes 4096 | tf_op jit(solution)/shard_map/psum | solution.py:67
  57.1 1.1 subtract_convert_fusion
  58.2 0.8 copy_bitcast_fusion
  59.0 2.3 convolution_convert_fusion.2
  61.4 35.7 %all-gather = s32[32,1,256]{2,1,0:T(1,128)S(1)} all-gather(s32[1,1,256]{2,1,0:T(1,128)S(1)} %bitcast.69), channel_id=1, replica_groups=mesh['req'=32,'mlp'=8] {'req'}, dimensions={0}, use_global_device_ids=true | all-gather | bytes 33792 | tf_op jit(solution)/shard_map/all_gather | solution.py:102
  97.3 40.7 %all-gather.10.cloned.1.call-done = bf16[8192,256]{1,0:T(8,128)(2,1)} async-done(((bf16[256,256]{1,0:T(8,128)(2,1)}), bf16[8192,256]{1,0:T(8,128)(2,1)}) %all-gather.10.cloned.1.call-update) | async-done | bytes 4194320 | tf_op jit(solution)/shard_map/all_gather | solution.py:100
  138.0 81.7 %all-gather.12.cloned.1.call-done = bf16[8192,256]{1,0:T(8,128)(2,1)} async-done(((bf16[256,256]{1,0:T(8,128)(2,1)}), bf16[8192,256]{1,0:T(8,128)(2,1)}) %all-gather.12.cloned.1.call-update) | async-done | bytes 4194320 | tf_op jit(solution)/shard_map/all_gather | solution.py:101
  219.7 44.8 %while.18 = (s32[]{:T(128)}, f32[2,256]{1,0:T(2,128)S(1)}, f32[2,256]{1,0:T(2,128)S(1)}, f32[256,2,128]{0,2,1:T(8,128)S(1)}, s32[256]{0:T(256)S(1)}, /*index=5*/...) while((s32[]{:T(128)}, f32[2,256]{1,0:T(2,128)S(1)}, ...), condition=%wide.region_11.12_spmd.clone, body=%wide.region_8.11_spmd.clone.sunk | while | flops 137302784 | bytes 6994131 | solution.py:142
  220.1 1.1 constant_dynamic-slice_fusion.3
  222.9 1.1 constant_dynamic-slice_fusion.3
  225.7 1.1 constant_dynamic-slice_fusion.3
  228.5 1.1 constant_dynamic-slice_fusion.3
  231.3 1.1 constant_dynamic-slice_fusion.3
  234.1 1.1 constant_dynamic-slice_fusion.3
  236.9 1.1 constant_dynamic-slice_fusion.3
  239.7 1.1 constant_dynamic-slice_fusion.3
  242.5 1.1 constant_dynamic-slice_fusion.3
  245.3 1.1 constant_dynamic-slice_fusion.3
  248.1 1.1 constant_dynamic-slice_fusion.3
  250.9 1.1 constant_dynamic-slice_fusion.3
  253.7 1.1 constant_dynamic-slice_fusion.3
  256.5 1.1 constant_dynamic-slice_fusion.3
  259.3 1.1 constant_dynamic-slice_fusion.3
  262.1 1.1 constant_dynamic-slice_fusion.3
  264.6 1.4 convolution_convert_fusion.1
  266.2 0.5 all-gather.14.cloned.1.call-update
  266.7 0.5 all-gather.16.cloned.1.call-update
  267.3 0.7 all-gather.18.cloned.1.call-update
  268.1 31.0 %reduce-scatter.3.cloned.1.call-done = bf16[256,256]{1,0:T(8,128)(2,1)} async-done(((bf16[256,2048]{1,0:T(8,128)(2,1)}), bf16[256,256]{1,0:T(8,128)(2,1)}) %reduce-scatter.3.cloned.1.call-update) | async-done | bytes 131088 | tf_op jit(solution)/shard_map/reduce_scatter | solution.py:35
  299.1 1.0 fusion.15
  300.1 14.9 %psum.38 = f32[256]{0:T(256)S(1)} all-reduce(f32[256]{0:T(256)S(1)} %fusion.15), channel_id=1, replica_groups=mesh['req'=32,'mlp'=8] {'mlp'}, use_global_device_ids=true, to_apply=%region_14.15 | all-reduce | flops 256 | bytes 2048 | tf_op jit(solution)/shard_map/psum | solution.py:38
  315.1 1.0 constant_dynamic-update-slice_fusion.7
  316.2 1.4 collective-permute-start.1
  317.6 0.8 collective-permute-done
  318.4 2.2 collective-permute-start.2
  320.6 0.4 collective-permute-done.1
  321.0 2.2 collective-permute-start.3
  323.2 0.8 collective-permute-done.2
  324.0 1.0 collective-permute-start.4
  325.0 0.7 collective-permute-done.3
  325.7 3.1 collective-permute-start.5
  328.8 0.8 collective-permute-done.4
  329.6 0.4 collective-permute-done.5
  330.1 5.2 collective-permute-done.6
  335.2 45.7 %all-gather.14.cloned.1.call-done = bf16[2048,1024]{1,0:T(8,128)(2,1)} async-done(((bf16[64,1024]{1,0:T(8,128)(2,1)}), bf16[2048,1024]{1,0:T(8,128)(2,1)}) %all-gather.14.cloned.1.call-update) | async-done | bytes 4194320 | tf_op jit(solution)/shard_map/all_gather | solution.py:189
  380.9 3.4 fusion.33
  384.4 77.5 %all-gather.16.cloned.1.call-done = bf16[2048,1024]{1,0:T(8,128)(2,1)} async-done(((bf16[64,1024]{1,0:T(8,128)(2,1)}), bf16[2048,1024]{1,0:T(8,128)(2,1)}) %all-gather.16.cloned.1.call-update) | async-done | bytes 4194320 | tf_op jit(solution)/shard_map/all_gather | solution.py:190
  462.0 81.2 %all-gather.18.cloned.1.call-done = bf16[2048,1024]{1,0:T(8,128)(2,1)} async-done(((bf16[64,1024]{1,0:T(8,128)(2,1)}), bf16[2048,1024]{1,0:T(8,128)(2,1)}) %all-gather.18.cloned.1.call-update) | async-done | bytes 4194320 | tf_op jit(solution)/shard_map/all_gather | solution.py:197
  543.1 7.0 %convolution_convert_fusion = bf16[256,2048]{1,0:T(8,128)(2,1)} fusion(bf16[2048,1024]{1,0:T(8,128)(2,1)} %all-gather.18.cloned.1.call-done, f32[256,1024]{1,0:T(8,128)S(1)} %fusion.33, bf16[256,2048]{1,0:T(8,128)(2,1)S(1)} %constant_dynamic-update-slice_fusion, bf16[2048,1024]{1,0:T(8,128)(2,1)} %all-gather.16.cloned.1.call-done), kind=kOutput, calls=%fused_computation.28 | convolution fusion | flops 2149580800 | bytes 11534336 | tf_op jit(solution)/shard_map/dot_general | solution.py:195
  550.4 3.7 gather_fusion
  554.1 3.7 gather_fusion.1
  557.8 0.8 maximum_select_fusion
  558.6 24.5 %reduce-scatter.5.cloned.1.call-done = bf16[256,256]{1,0:T(8,128)(2,1)} async-done(((bf16[256,2048]{1,0:T(8,128)(2,1)}), bf16[256,256]{1,0:T(8,128)(2,1)}) %reduce-scatter.5.cloned.1.call-update) | async-done | bytes 131088 | tf_op jit(solution)/shard_map/reduce_scatter | solution.py:35
  583.1 1.0 fusion.19
  584.1 14.8 %psum.39 = f32[256]{0:T(256)S(1)} all-reduce(f32[256]{0:T(256)S(1)} %fusion.19), channel_id=1, replica_groups=mesh['req'=32,'mlp'=8] {'mlp'}, use_global_device_ids=true, to_apply=%region_17.18 | all-reduce | flops 256 | bytes 2048 | tf_op jit(solution)/shard_map/psum | solution.py:38
  598.9 1.7 fusion.22
  (275 shorter events, 28.4 us)
Async XLA Ops:
  7.2 257.5 %copy-start = (bf16[256,2048]{1,0:T(8,128)(2,1)S(1)}, bf16[256,2048]{1,0:T(8,128)(2,1)}, u32[]{:S(2)}) copy-start(bf16[256,2048]{1,0:T(8,128)(2,1)} %param.22) | copy-start | bytes 3145732
  7.2 49.1 %copy-start.4 = (f32[256]{0:T(256)S(1)}, f32[256]{0:T(256)}, u32[]{:S(2)}) copy-start(f32[256]{0:T(256)} %param.24) | copy-start | bytes 3076
  7.2 49.5 %copy-start.5 = (f32[256]{0:T(256)S(1)}, f32[256]{0:T(256)}, u32[]{:S(2)}) copy-start(f32[256]{0:T(256)} %param.23) | copy-start | bytes 3076
  7.2 32.8 %all-gather.8.cloned.1.call-start = ((), (), s32[]{:S(2)}) async-start(), calls=%async_computation.2 | async-start | bytes 1179648 | tf_op jit(solution)/shard_map/all_gather | solution.py:63
  7.9 130.0 %all-gather.10.cloned.1.call-start = ((), (), s32[]{:S(2)}) async-start(), calls=%async_computation.3 | async-start | bytes 4325376 | tf_op jit(solution)/shard_map/all_gather | solution.py:100
  42.0 17.0 %copy-start.1 = (bf16[256,2048]{1,0:T(8,128)(2,1)S(1)}, bf16[256,2048]{1,0:T(8,128)(2,1)}, u32[]{:S(2)}) copy-start(bf16[256,2048]{1,0:T(8,128)(2,1)} %all-gather.8.cloned.1.call-done) | copy-start | bytes 3145732
  56.3 5.1 copy-start.3
  58.9 160.8 %all-gather.12.cloned.1.call-start = ((), (), s32[]{:S(2)}) async-start(), calls=%async_computation.4 | async-start | bytes 4325376 | tf_op jit(solution)/shard_map/all_gather | solution.py:101
  61.4 237.7 %reduce-scatter.3.cloned.1.call-start = ((), (), s32[]{:S(2)}) async-start(), calls=%async_computation.5 | async-start | bytes 1179648 | tf_op jit(solution)/shard_map/reduce_scatter | solution.py:35
  264.6 50.6 %copy-start.2 = (bf16[256,256]{1,0:T(8,128)(2,1)S(1)}, bf16[256,256]{1,0:T(8,128)(2,1)}, u32[]{:S(2)}) copy-start(bf16[256,256]{1,0:T(8,128)(2,1)} %param.16) | copy-start | bytes 393220
  264.6 50.6 %copy-start.6 = (f32[256]{0:T(256)S(1)}, f32[256]{0:T(256)}, u32[]{:S(2)}) copy-start(f32[256]{0:T(256)} %param.25) | copy-start | bytes 3076
  266.1 114.8 %all-gather.14.cloned.1.call-start = ((), (), s32[]{:S(2)}) async-start(), calls=%async_computation.6 | async-start | bytes 4325376 | tf_op jit(solution)/shard_map/all_gather | solution.py:189
  266.7 195.3 %all-gather.16.cloned.1.call-start = ((), (), s32[]{:S(2)}) async-start(), calls=%async_computation.7 | async-start | bytes 4325376 | tf_op jit(solution)/shard_map/all_gather | solution.py:190
  267.3 275.8 %all-gather.18.cloned.1.call-start = ((), (), s32[]{:S(2)}) async-start(), calls=%async_computation.8 | async-start | bytes 4325376 | tf_op jit(solution)/shard_map/all_gather | solution.py:197
  268.0 315.1 %reduce-scatter.5.cloned.1.call-start = ((), (), s32[]{:S(2)}) async-start(), calls=%async_computation.9 | async-start | bytes 1179648 | tf_op jit(solution)/shard_map/reduce_scatter | solution.py:35
  316.2 2.2 collective-permute-start
  316.2 4.8 collective-permute-start.1
  318.4 5.6 collective-permute-start.2
  321.0 4.6 collective-permute-start.3
  324.0 5.6 collective-permute-start.4
  325.7 4.4 collective-permute-start.5
  329.6 5.6 collective-permute-start.6
  384.4 165.7 %copy-start.8 = (s32[16]{0:T(128)S(1)}, s32[16]{0:T(128)}, u32[]{:S(2)}) copy-start(s32[16]{0:T(128)} %param.18) | copy-start | bytes 196
  384.4 214.5 %copy-start.7 = (f32[256]{0:T(256)S(1)}, f32[256]{0:T(256)}, u32[]{:S(2)}) copy-start(f32[256]{0:T(256)} %param.29) | copy-start | bytes 3076
Sparse Core Ops, SparseCore 0:
  9.8 30.0 all-gather.7
  59.1 78.8 all-gather.9
  141.1 78.5 all-gather.11
  266.2 32.7 reduce-scatter.2
  301.5 79.4 all-gather.13
  383.4 78.5 all-gather.15
  464.5 78.5 all-gather.17
  550.2 32.8 reduce-scatter.4
